TPU v7x, 32 devices: a whole 2x2x4 slice. The times are simulated.
32 devices in a mesh: pipe: 2 (over x), expert: 16 (over z, y, core).
Axes of the slice: x: 2, y: 2, z: 4, core: 2. Of those that a mesh axis runs over, the one named last changes fastest.
Arguments:
- inputs: bfloat16 [1, 512, 5120], P(None, 'expert'), may hold values from -6 to 6
- router: bfloat16 [2, 5120, 2], P('pipe'), may hold values from -0.078125 to 0.078125
- w_up: bfloat16 [2, 3072, 5120], P('pipe', 'expert'), may hold values from -0.078125 to 0.078125
- w_down: bfloat16 [2, 3072, 5120], P('pipe', 'expert'), may hold values from -0.15625 to 0.15625
- picks: int32 [2, 1, 2, 8], P('pipe'), may hold values from 0 to 511, as said below
- probe: bfloat16 [2, 64, 5120], P('pipe'), may hold values from -0.078125 to 0.078125
Outputs:
- student_feats: bfloat16 [2, 1, 512, 64], P('pipe', None, 'expert')
Inputs may be any that keep to these rules, and one draw needn't show every extreme that they name: Each list picks[s, m, e] holds 8 different token positions of the micro-batch. Of the 32 consecutive positions held by one index of expert, at most 1 stand in one list, and in every list some index has exactly 1.
All inputs are finite; a program needn't handle non-finite values.
Results may differ from a plain program's by a relative error of at most 0.0059.
Values may be sent and summed in bfloat16 or wider, within the bound.
A program may use at most 64 MiB of HBM per device.

v0:
```python
import jax
import jax.numpy as jnp
from jax import lax
from jax.sharding import PartitionSpec as P

SLOT = 1


def passed_along(x, axis, by):
    size = lax.axis_size(axis)
    pairs = [(i, i + by) for i in range(size) if 0 <= i + by < size]
    return lax.ppermute(x, axis, pairs)


def from_root(x, axis, root):
    mine = lax.axis_index(axis) == root
    return lax.psum(jnp.where(mine, x, jnp.zeros_like(x)), axis)


def rms_rows(rows_in):
    wide = rows_in.astype(jnp.float32)
    scale = lax.rsqrt(jnp.mean(wide * wide, axis=-1, keepdims=True) + 1e-06)
    return (wide * scale).astype(jnp.bfloat16)


def shards(inputs, router, w_up, w_down, picks, probe):
    sections = lax.axis_size("pipe")
    expert_width = lax.axis_size("expert")
    section_index = lax.axis_index("pipe")
    source = lax.axis_index("expert")
    micro_count, tok_rows, features = inputs.shape
    experts = router.shape[2]
    group_size = expert_width // experts
    tick_count = micro_count + sections - 1
    positions = jnp.arange(tok_rows, dtype=jnp.int32)
    slot_ids = jnp.arange(SLOT, dtype=jnp.int32)

    def expert_rows(received):
        row_shape = received.shape
        flat_rows = received.reshape(-1, row_shape[2])
        pre = lax.dot_general(
            flat_rows, w_up[0], (((1,), (1,)), ((), ())), preferred_element_type=jnp.float32
        )
        hidden = jax.nn.silu(pre).astype(jnp.bfloat16)
        partials = jnp.dot(hidden, w_down[0], preferred_element_type=jnp.float32).astype(
            jnp.bfloat16
        )
        return partials.reshape(row_shape)

    def layer(rows_in, micro_index):
        normed = rms_rows(rows_in)
        gate_values = jax.nn.sigmoid(jnp.dot(normed, router[0], preferred_element_type=jnp.float32))
        chosen = lax.dynamic_index_in_dim(picks[0], micro_index, 0, keepdims=False)
        local_rows = chosen - source * tok_rows
        owned = (local_rows >= 0) & (local_rows < tok_rows)
        owned_count = owned.astype(jnp.int32)
        slot_place = jnp.cumsum(owned_count, axis=1) - owned_count
        slot_hot = ((slot_place[:, :, None] == slot_ids) & owned[:, :, None]).astype(jnp.bfloat16)
        row_hot = (local_rows[:, :, None] == positions).astype(jnp.bfloat16)
        selector = jnp.einsum("ecr,ect->ert", slot_hot, row_hot, preferred_element_type=jnp.float32)
        picked = jnp.einsum(
            "ert,td->erd", selector.astype(jnp.bfloat16), normed, preferred_element_type=jnp.float32
        ).astype(jnp.bfloat16)
        copies = jnp.repeat(picked, group_size, axis=0)
        partials = expert_rows(
            lax.all_to_all(copies, "expert", split_axis=0, concat_axis=0, tiled=True)
        )
        returned = lax.all_to_all(partials, "expert", split_axis=0, concat_axis=0, tiled=True)
        expert_out = jnp.sum(
            returned.astype(jnp.float32).reshape(experts, group_size, SLOT, features), axis=1
        )
        weights = selector * jnp.transpose(gate_values)[:, None, :]
        update = jnp.einsum("ert,erd->td", weights, expert_out, precision=lax.Precision.HIGHEST)
        return (rows_in.astype(jnp.float32) + update).astype(jnp.bfloat16)

    def tick(tick_index, loop_state):
        previous, finals = loop_state
        arrived = passed_along(previous, "pipe", 1)
        micro_index = jnp.clip(tick_index - section_index, 0, micro_count - 1)
        fresh_rows = lax.dynamic_index_in_dim(
            inputs, jnp.clip(tick_index, 0, micro_count - 1), 0, keepdims=False
        )
        rows_in = jnp.where(section_index == 0, fresh_rows, arrived)
        result = layer(rows_in, micro_index)
        finished = (
            (section_index == sections - 1)
            & (tick_index - section_index >= 0)
            & (tick_index - section_index < micro_count)
        )
        stored = lax.dynamic_update_index_in_dim(finals, result, micro_index, 0)
        finals = jnp.where(finished, stored, finals)
        return (result, finals)

    start_rows = jnp.zeros((tok_rows, features), jnp.bfloat16)
    start_finals = jnp.zeros((micro_count, tok_rows, features), jnp.bfloat16)
    previous, finals = lax.fori_loop(0, tick_count, tick, (start_rows, start_finals))
    shared = from_root(finals, "pipe", sections - 1)
    final_normed = rms_rows(shared)
    student_rows = jnp.einsum(
        "mtd,jd->mtj", final_normed, probe[0], preferred_element_type=jnp.float32
    )
    return student_rows.astype(jnp.bfloat16)[None]


def solution(mesh):
    return jax.shard_map(
        shards,
        mesh=mesh,
        in_specs=(
            P(None, "expert", None),
            P("pipe", None, None),
            P("pipe", "expert", None),
            P("pipe", "expert", None),
            P("pipe", None, None, None),
            P("pipe", None, None),
        ),
        out_specs=P("pipe", None, "expert", None),
        check_vma=False,
    )
```

profile of v0, /device:TPU:0, one launch (start us, length us, event | category | flops | bytes accessed | tf_op | source)
XLA Modules:
  0.0 138.6 jit_solution(14568044816781589299)
XLA Ops:
  6.5 0.0 copy-start
  6.5 0.0 all-reduce.2.cloned.1.call-start
  6.5 0.7 fusion.38
  7.3 0.2 reduce_window_sum.19
  7.5 0.2 fusion.35
  7.7 95.9 %while.21 = (s32[]{:T(128)}, bf16[32,5120]{1,0:T(8,128)(2,1)}, bf16[1,32,5120]{2,1,0:T(8,128)(2,1)}, pred[]{:T(512)}, bf16[1,32,5120]{2,1,0:T(8,128)(2,1)}, /*in...) while((s32[]{:T(128)}, bf16[32,5120]{1,0:T(8,128)(2,1)}, ...), condition=%wide.region_4.5_spmd.clone, body=%wide.region_1.4_spmd.clone.sunk | while | flops 71040296 | bytes 23656336 | solution.py:96
  7.7 0.0 copy-start.1
  7.7 5.0 %collective-permute-start = (bf16[32,5120]{1,0:T(8,128)(2,1)S(1)}, bf16[32,5120]{1,0:T(8,128)(2,1)S(1)}, u32[]{:S(2)}, u32[]{:S(2)}) collective-permute-start(bf16[32,5120]{1,0:T(8,128)(2,1)S(1)} %broadcast_select_fusion.3), channel_id=1, source_target_pairs={{0,16},{1,17},{2,18},{3,19},{4,20},{5,21},{6,22},{7,23},{8,24},{9,... | collective-permute-start | bytes 983048 | tf_op jit(solution)/shard_map/while/body/eval_jaxpr/ppermute | solution.py:12
  12.7 6.9 %collective-permute-done = bf16[32,5120]{1,0:T(8,128)(2,1)S(1)} collective-permute-done((bf16[32,5120]{1,0:T(8,128)(2,1)S(1)}, bf16[32,5120]{1,0:T(8,128)(2,1)S(1)}, u32[]{:S(2)}, u32[]{:S(2)}) %collective-permute-start) | collective-permute-done | bytes 327712 | tf_op jit(solution)/shard_map/while/body/eval_jaxpr/ppermute | solution.py:12
  19.7 1.2 fusion.64
  20.9 0.2 fusion.65
  21.2 0.6 broadcast.199
  21.8 0.8 reduce.13
  22.5 0.1 reshape.138
  22.6 14.2 %all_to_all.32 = bf16[16,2,2560]{2,1,0:T(2,128)(2,1)S(1)} all-to-all(bf16[16,2,2560]{2,1,0:T(2,128)(2,1)S(1)} %reshape.138), channel_id=1, replica_groups=mesh['pipe'=2,'expert'=16] {'expert'}, dimensions={0} | all-to-all | bytes 327680 | tf_op jit(solution)/shard_map/while/body/eval_jaxpr/all_to_all | solution.py:66
  36.8 0.1 reshape.139
  36.9 0.0 copy-done.1
  36.9 0.0 copy-start.4
  37.0 3.0 %fusion.66 = bf16[16,1,5120]{2,0,1:T(8,128)(2,1)S(1)} fusion(bf16[1,192,5120]{2,1,0:T(8,128)(2,1)} %get-tuple-element.587, bf16[1,192,5120]{2,1,0:T(8,128)(2,1)S(1)} %copy-done.1, bf16[16,1,5120]{2,1,0:T(2,128)(2,1)S(1)} %reshape.139), kind=kOutput, calls=%fused_computation.3.clone.1 | convolution fusion | flops 63011840 | bytes 4259840 | tf_op jit(solution)/shard_map/while/body/eval_jaxpr/dot_general | solution.py:45
  40.0 0.6 broadcast.200
  40.6 0.8 reduce.14
  41.4 0.8 reshape.140
  42.1 3.5 %all-to-all-start.1 = ((bf16[16,2,2560]{2,1,0:T(2,128)(2,1)}), bf16[16,2,2560]{2,1,0:T(2,128)(2,1)S(1)}, u32[]{:S(2)}, u32[]{:S(2)}) async-start(bf16[16,2,2560]{2,1,0:T(2,128)(2,1)} %reshape.140), calls=%async_computation.1 | async-start | bytes 327680 | tf_op jit(solution)/shard_map/while/body/eval_jaxpr/all_to_all | solution.py:68
  45.7 0.0 copy-done.4
  45.7 0.3 fusion.67
  45.9 8.1 %all-to-all-done.1 = bf16[16,2,2560]{2,1,0:T(2,128)(2,1)S(1)} async-done(((bf16[16,2,2560]{2,1,0:T(2,128)(2,1)}), bf16[16,2,2560]{2,1,0:T(2,128)(2,1)S(1)}, u32[]{:S(2)}, u32[]{:S(2)}) %all-to-all-start.1) | async-done | bytes 163872 | tf_op jit(solution)/shard_map/while/body/eval_jaxpr/all_to_all | solution.py:68
  54.0 0.1 reshape.141
  54.2 0.3 reshape.142
  54.5 0.1 bitcast_reduce_fusion.2
  54.7 0.0 copy-done.2
  54.7 1.6 %bitcast_select_fusion.4 = (bf16[1,32,5120]{2,1,0:T(8,128)(2,1)S(1)}, bf16[32,5120]{1,0:T(8,128)(2,1)}) fusion(bf16[1,32,5120]{2,1,0:T(8,128)(2,1)S(1)} %copy-done.2, pred[]{:T(512)S(6)} %compare.3, pred[]{:T(512)S(6)} %and.69, f32[2,32]{1,0:T(2,128)S(1)} %fusion.67, f32[2,5120]{1,0:T(2,128)S(1)} %bitcast_reduce_fusion.2, ...), kind=kOutput, calls=%fused_computation.20.clone.1 | convolution fusion | flops 4751360 | bytes 1351938 | tf_op jit(solution)/shard_map/while/body/eval_jaxpr/ert,erd->td/dot_general | solution.py:73
  56.2 0.7 copy-done.3
  57.0 1.1 broadcast_select_fusion.3
  58.1 4.4 %collective-permute-start = (bf16[32,5120]{1,0:T(8,128)(2,1)S(1)}, bf16[32,5120]{1,0:T(8,128)(2,1)S(1)}, u32[]{:S(2)}, u32[]{:S(2)}) collective-permute-start(bf16[32,5120]{1,0:T(8,128)(2,1)S(1)} %broadcast_select_fusion.3), channel_id=1, source_target_pairs={{0,16},{1,17},{2,18},{3,19},{4,20},{5,21},{6,22},{7,23},{8,24},{9,... | collective-permute-start | bytes 983048 | tf_op jit(solution)/shard_map/while/body/eval_jaxpr/ppermute | solution.py:12
  62.5 6.3 %collective-permute-done = bf16[32,5120]{1,0:T(8,128)(2,1)S(1)} collective-permute-done((bf16[32,5120]{1,0:T(8,128)(2,1)S(1)}, bf16[32,5120]{1,0:T(8,128)(2,1)S(1)}, u32[]{:S(2)}, u32[]{:S(2)}) %collective-permute-start) | collective-permute-done | bytes 327712 | tf_op jit(solution)/shard_map/while/body/eval_jaxpr/ppermute | solution.py:12
  68.9 1.2 fusion.64
  70.1 0.2 fusion.65
  70.4 0.6 broadcast.199
  71.0 0.8 reduce.13
  71.7 0.1 reshape.138
  71.8 11.6 %all_to_all.32 = bf16[16,2,2560]{2,1,0:T(2,128)(2,1)S(1)} all-to-all(bf16[16,2,2560]{2,1,0:T(2,128)(2,1)S(1)} %reshape.138), channel_id=1, replica_groups=mesh['pipe'=2,'expert'=16] {'expert'}, dimensions={0} | all-to-all | bytes 327680 | tf_op jit(solution)/shard_map/while/body/eval_jaxpr/all_to_all | solution.py:66
  83.4 0.1 reshape.139
  83.6 0.0 copy-done.1
  83.6 0.0 copy-start.4
  83.6 3.0 %fusion.66 = bf16[16,1,5120]{2,0,1:T(8,128)(2,1)S(1)} fusion(bf16[1,192,5120]{2,1,0:T(8,128)(2,1)} %get-tuple-element.587, bf16[1,192,5120]{2,1,0:T(8,128)(2,1)S(1)} %copy-done.1, bf16[16,1,5120]{2,1,0:T(2,128)(2,1)S(1)} %reshape.139), kind=kOutput, calls=%fused_computation.3.clone.1 | convolution fusion | flops 63011840 | bytes 4259840 | tf_op jit(solution)/shard_map/while/body/eval_jaxpr/dot_general | solution.py:45
  86.6 0.6 broadcast.200
  87.2 0.8 reduce.14
  88.0 0.8 reshape.140
  88.7 3.5 %all-to-all-start.1 = ((bf16[16,2,2560]{2,1,0:T(2,128)(2,1)}), bf16[16,2,2560]{2,1,0:T(2,128)(2,1)S(1)}, u32[]{:S(2)}, u32[]{:S(2)}) async-start(bf16[16,2,2560]{2,1,0:T(2,128)(2,1)} %reshape.140), calls=%async_computation.1 | async-start | bytes 327680 | tf_op jit(solution)/shard_map/while/body/eval_jaxpr/all_to_all | solution.py:68
  92.3 0.0 copy-done.4
  92.3 0.3 fusion.67
  92.6 8.1 %all-to-all-done.1 = bf16[16,2,2560]{2,1,0:T(2,128)(2,1)S(1)} async-done(((bf16[16,2,2560]{2,1,0:T(2,128)(2,1)}), bf16[16,2,2560]{2,1,0:T(2,128)(2,1)S(1)}, u32[]{:S(2)}, u32[]{:S(2)}) %all-to-all-start.1) | async-done | bytes 163872 | tf_op jit(solution)/shard_map/while/body/eval_jaxpr/all_to_all | solution.py:68
  100.7 0.1 reshape.141
  100.8 0.3 reshape.142
  101.1 0.1 bitcast_reduce_fusion.2
  101.3 0.0 copy-done.2
  101.3 1.6 %bitcast_select_fusion.4 = (bf16[1,32,5120]{2,1,0:T(8,128)(2,1)S(1)}, bf16[32,5120]{1,0:T(8,128)(2,1)}) fusion(bf16[1,32,5120]{2,1,0:T(8,128)(2,1)S(1)} %copy-done.2, pred[]{:T(512)S(6)} %compare.3, pred[]{:T(512)S(6)} %and.69, f32[2,32]{1,0:T(2,128)S(1)} %fusion.67, f32[2,5120]{1,0:T(2,128)S(1)} %bitcast_reduce_fusion.2, ...), kind=kOutput, calls=%fused_computation.20.clone.1 | convolution fusion | flops 4751360 | bytes 1351938 | tf_op jit(solution)/shard_map/while/body/eval_jaxpr/ert,erd->td/dot_general | solution.py:73
  102.9 0.7 copy-done.3
  103.6 0.7 broadcast_select_fusion.1
  104.3 0.0 all-reduce.2.cloned.1.call-update
  104.4 24.3 %all-reduce.2.cloned.1.call-done = bf16[1,32,5120]{2,1,0:T(8,128)(2,1)} async-done(((bf16[1,32,5120]{2,1,0:T(8,128)(2,1)}), bf16[1,32,5120]{2,1,0:T(8,128)(2,1)}) %all-reduce.2.cloned.1.call-update) | async-done | bytes 327696 | tf_op jit(solution)/shard_map/psum | solution.py:17
  128.6 1.1 fusion.29
  129.8 0.0 copy-done
  129.8 1.9 %fusion.28 = bf16[1,1,32,64]{3,2,1,0:T(8,128)(2,1)} fusion(bf16[1,64,5120]{2,1,0:T(8,128)(2,1)S(1)} %copy-done, bf16[1,32,5120]{2,1,0:T(8,128)(2,1)} %all-reduce.2.cloned.1.call-done, f32[32]{0:T(128)S(1)} %add_rsqrt_fusion.1), kind=kOutput, calls=%fused_computation.32 | convolution fusion | flops 21465088 | bytes 987264 | tf_op jit(solution)/shard_map/mtd,jd->mtj/dot_general | solution.py:99
  (15 shorter events, 0.1 us)
Async XLA Ops:
  6.5 123.3 %copy-start = (bf16[1,64,5120]{2,1,0:T(8,128)(2,1)S(1)}, bf16[1,64,5120]{2,1,0:T(8,128)(2,1)}, u32[]{:S(2)}) copy-start(bf16[1,64,5120]{2,1,0:T(8,128)(2,1)} %param.13) | copy-start | bytes 1966084
  6.5 122.1 %all-reduce.2.cloned.1.call-start = ((), (), s32[]{:S(2)}) async-start(), calls=%async_computation.2 | async-start | bytes 655360 | tf_op jit(solution)/shard_map/psum | solution.py:17
  7.7 29.3 %copy-start.1 = (bf16[1,192,5120]{2,1,0:T(8,128)(2,1)S(1)}, bf16[1,192,5120]{2,1,0:T(8,128)(2,1)}, u32[]{:S(2)}) copy-start(bf16[1,192,5120]{2,1,0:T(8,128)(2,1)} %get-tuple-element.586) | copy-start | bytes 5898244 | tf_op jit(solution)/shard_map/while
  7.7 12.0 %collective-permute-start = (bf16[32,5120]{1,0:T(8,128)(2,1)S(1)}, bf16[32,5120]{1,0:T(8,128)(2,1)S(1)}, u32[]{:S(2)}, u32[]{:S(2)}) collective-permute-start(bf16[32,5120]{1,0:T(8,128)(2,1)S(1)} %broadcast_select_fusion.3), channel_id=1, source_target_pairs={{0,16},{1,17},{2,18},{3,19},{4,20},{5,21},{6,22},{7,23},{8,24},{9,... | collective-permute-start | bytes 983048 | tf_op jit(solution)/shard_map/while/body/eval_jaxpr/ppermute | solution.py:12
  36.9 8.7 %copy-start.4 = (bf16[1,5120,2]{1,2,0:T(2,128)(2,1)S(1)}, bf16[1,5120,2]{1,2,0:T(2,128)(2,1)}, u32[]{:S(2)}) copy-start(bf16[1,5120,2]{1,2,0:T(2,128)(2,1)} %get-tuple-element.583) | copy-start | bytes 61444 | tf_op jit(solution)/shard_map/while
  40.0 14.7 %copy-start.2 = (bf16[1,32,5120]{2,1,0:T(8,128)(2,1)S(1)}, bf16[1,32,5120]{2,1,0:T(8,128)(2,1)}, u32[]{:S(2)}) copy-start(bf16[1,32,5120]{2,1,0:T(8,128)(2,1)} %get-tuple-element.564) | copy-start | bytes 983044 | tf_op jit(solution)/shard_map/while
  42.1 11.9 %all-to-all-start.1 = ((bf16[16,2,2560]{2,1,0:T(2,128)(2,1)}), bf16[16,2,2560]{2,1,0:T(2,128)(2,1)S(1)}, u32[]{:S(2)}, u32[]{:S(2)}) async-start(bf16[16,2,2560]{2,1,0:T(2,128)(2,1)} %reshape.140), calls=%async_computation.1 | async-start | bytes 327680 | tf_op jit(solution)/shard_map/while/body/eval_jaxpr/all_to_all | solution.py:68
  56.2 0.7 copy-start.3
  57.0 26.6 %copy-start.1 = (bf16[1,192,5120]{2,1,0:T(8,128)(2,1)S(1)}, bf16[1,192,5120]{2,1,0:T(8,128)(2,1)}, u32[]{:S(2)}) copy-start(bf16[1,192,5120]{2,1,0:T(8,128)(2,1)} %get-tuple-element.586) | copy-start | bytes 5898244 | tf_op jit(solution)/shard_map/while
  58.1 10.8 %collective-permute-start = (bf16[32,5120]{1,0:T(8,128)(2,1)S(1)}, bf16[32,5120]{1,0:T(8,128)(2,1)S(1)}, u32[]{:S(2)}, u32[]{:S(2)}) collective-permute-start(bf16[32,5120]{1,0:T(8,128)(2,1)S(1)} %broadcast_select_fusion.3), channel_id=1, source_target_pairs={{0,16},{1,17},{2,18},{3,19},{4,20},{5,21},{6,22},{7,23},{8,24},{9,... | collective-permute-start | bytes 983048 | tf_op jit(solution)/shard_map/while/body/eval_jaxpr/ppermute | solution.py:12
  83.6 8.7 %copy-start.4 = (bf16[1,5120,2]{1,2,0:T(2,128)(2,1)S(1)}, bf16[1,5120,2]{1,2,0:T(2,128)(2,1)}, u32[]{:S(2)}) copy-start(bf16[1,5120,2]{1,2,0:T(2,128)(2,1)} %get-tuple-element.583) | copy-start | bytes 61444 | tf_op jit(solution)/shard_map/while
  86.6 14.7 %copy-start.2 = (bf16[1,32,5120]{2,1,0:T(8,128)(2,1)S(1)}, bf16[1,32,5120]{2,1,0:T(8,128)(2,1)}, u32[]{:S(2)}) copy-start(bf16[1,32,5120]{2,1,0:T(8,128)(2,1)} %get-tuple-element.564) | copy-start | bytes 983044 | tf_op jit(solution)/shard_map/while
  88.7 11.9 %all-to-all-start.1 = ((bf16[16,2,2560]{2,1,0:T(2,128)(2,1)}), bf16[16,2,2560]{2,1,0:T(2,128)(2,1)S(1)}, u32[]{:S(2)}, u32[]{:S(2)}) async-start(bf16[16,2,2560]{2,1,0:T(2,128)(2,1)} %reshape.140), calls=%async_computation.1 | async-start | bytes 327680 | tf_op jit(solution)/shard_map/while/body/eval_jaxpr/all_to_all | solution.py:68
  102.9 0.7 copy-start.3
Sparse Core Ops, SparseCore 0:
  104.5 24.1 all-reduce.1
where the time goes:
time: 139 us
  waiting for transfers between devices  53.8 us (39%)
  blocking collectives  25.8 us (19%)
  starting transfers between devices  16.5 us (12%)
  between operations  13.4 us (10%)
  matrix products  12.4 us (9%)
  other arithmetic  10.4 us (7%)
  local copies, waits for them, and re-layouts  6.15 us (4%)
    all_to_all x2, blocking collectives, layer(): lax.all_to_all(copies, 'expert', split_axis=0, concat_axis=0, tiled=True)  25.8 us
    psum x1, waiting for transfers between devices, from_root(): return lax.psum(jnp.where(mine, x, jnp.zeros_like(x)), axis)  24.3 us
    all_to_all x2, waiting for transfers between devices, layer(): lax.all_to_all(partials, 'expert', split_axis=0, concat_axis=0, tiled=True)  16.2 us
    ppermute x2, waiting for transfers between devices, passed_along(): return lax.ppermute(x, axis, pairs)  13.3 us
    ppermute x2, starting transfers between devices, passed_along(): return lax.ppermute(x, axis, pairs)  9.43 us
    all_to_all x2, starting transfers between devices, layer(): lax.all_to_all(partials, 'expert', split_axis=0, concat_axis=0, tiled=True)  7.03 us
    dot_general x2, matrix products, expert_rows(): jnp.dot(hidden, w_down[0], preferred_element_type=jnp.float32)  6.05 us
    while x24, local copies, waits for them, and re-layouts  3.7 us
  transfers between devices with their start and end apart: 5, of which 5 were waited for; matrix products, arithmetic and copies ran while one was open for 0% of the time, Pallas kernels for 0%

commit v1 on v0

--- a/solution.py
+++ b/solution.py
@@ -4,6 +4,22 @@
 from jax.sharding import PartitionSpec as P
 
 SLOT = 1
+
+
+def swapped_with_each(x, axis, split, join):
+    ways, here = (lax.axis_size(axis), lax.axis_index(axis))
+    width = x.shape[split] // ways
+    shape = list(x.shape)
+    shape[split] = width
+    height = shape[join]
+    shape[join] = height * ways
+    full = jnp.zeros(shape, x.dtype)
+    for mask in range(ways):
+        part = lax.dynamic_slice_in_dim(x, (here ^ mask) * width, width, axis=split)
+        if mask:
+            part = lax.ppermute(part, axis, [(d, d ^ mask) for d in range(ways)])
+        full = lax.dynamic_update_slice_in_dim(full, part, (here ^ mask) * height, axis=join)
+    return full
 
 
 def passed_along(x, axis, by):
@@ -62,9 +78,7 @@
             "ert,td->erd", selector.astype(jnp.bfloat16), normed, preferred_element_type=jnp.float32
         ).astype(jnp.bfloat16)
         copies = jnp.repeat(picked, group_size, axis=0)
-        partials = expert_rows(
-            lax.all_to_all(copies, "expert", split_axis=0, concat_axis=0, tiled=True)
-        )
+        partials = expert_rows(swapped_with_each(copies, "expert", 0, 0))
         returned = lax.all_to_all(partials, "expert", split_axis=0, concat_axis=0, tiled=True)
         expert_out = jnp.sum(
             returned.astype(jnp.float32).reshape(experts, group_size, SLOT, features), axis=1

time: 139 us -> 161 us (1.16)
  starting transfers between devices: 16.5 us -> 58.7 us
  blocking collectives: 25.8 us -> 0 us
  local copies, waits for them, and re-layouts: 6.15 us -> 14.2 us
  other arithmetic: 10.4 us -> 7.52 us
    ppermute x0 -> x30, starting transfers between devices: none -> 41.2 us  [swapped_with_each(): part = lax.ppermute(part, axis, [(d, d ^ mask) for d in range(ways)])]
    all_to_all x2 -> x0, blocking collectives: 25.8 us -> none  [layer(): lax.all_to_all(copies, 'expert', split_axis=0, concat_axis=0, tiled=True)]
    dynamic_update_slice x0 -> x32, local copies, waits for them, and re-layouts: none -> 9.1 us  [swapped_with_each(): lax.dynamic_update_slice_in_dim(full, part, (here ^ mask) * height, axis=...]
    while x24 -> x20, local copies, waits for them, and re-layouts: 3.7 us -> 3.23 us
  transfers between devices with their start and end apart: 5 -> 35, of which waited for: 5 -> 6; matrix products, arithmetic and copies ran while one was open for 0% -> 6% of each run, Pallas kernels for 0% -> 0%
where the time goes in v1:
time: 161 us
  starting transfers between devices  58.7 us (36%)
  waiting for transfers between devices  55 us (34%)
  local copies, waits for them, and re-layouts  14.2 us (9%)
  between operations  13.4 us (8%)
  matrix products  11 us (7%)
  other arithmetic  7.52 us (5%)
    ppermute x30, starting transfers between devices, swapped_with_each(): part = lax.ppermute(part, axis, [(d, d ^ mask) for d in range(ways)])  41.2 us
    psum x1, waiting for transfers between devices, from_root(): return lax.psum(jnp.where(mine, x, jnp.zeros_like(x)), axis)  24.3 us
    all_to_all x2, waiting for transfers between devices, layer(): lax.all_to_all(partials, 'expert', split_axis=0, concat_axis=0, tiled=True)  16.2 us
    ppermute x2, waiting for transfers between devices, passed_along(): return lax.ppermute(x, axis, pairs)  13.1 us
    ppermute x2, starting transfers between devices, passed_along(): return lax.ppermute(x, axis, pairs)  9.56 us
    dynamic_update_slice x32, local copies, waits for them, and re-layouts, swapped_with_each(): lax.dynamic_update_slice_in_dim(full, part, (here ^ mask) * height, axis=...  9.1 us
    all_to_all x2, starting transfers between devices, layer(): lax.all_to_all(partials, 'expert', split_axis=0, concat_axis=0, tiled=True)  8.02 us
    dot_general x2, matrix products, expert_rows(): jnp.dot(hidden, w_down[0], preferred_element_type=jnp.float32)  6.06 us
  transfers between devices with their start and end apart: 35, of which 6 were waited for; matrix products, arithmetic and copies ran while one was open for 6% of the time, Pallas kernels for 0%

profile of v1, /device:TPU:0, one launch (start us, length us, event | category | flops | bytes accessed | tf_op | source)
XLA Modules:
  0.0 160.7 jit_solution(10407103792041353097)
XLA Ops:
  6.5 0.7 fusion.32
  7.7 118.0 %while.21 = (s32[]{:T(128)}, bf16[32,5120]{1,0:T(8,128)(2,1)S(1)}, bf16[1,32,5120]{2,1,0:T(8,128)(2,1)}, pred[]{:T(512)}, bf16[1,32,5120]{2,1,0:T(8,128)(2,1)}, ...) while((s32[]{:T(128)}, bf16[32,5120]{1,0:T(8,128)(2,1)S(1)}, ...), condition=%wide.region_4.5_spmd.clone, body=%wide.region_1.4_spmd.clone.sunk | while | flops 71040360 | bytes 23944652 | solution.py:110
  7.7 5.0 %collective-permute-start = (bf16[32,5120]{1,0:T(8,128)(2,1)S(1)}, bf16[32,5120]{1,0:T(8,128)(2,1)S(1)}, u32[]{:S(2)}, u32[]{:S(2)}) collective-permute-start(bf16[32,5120]{1,0:T(8,128)(2,1)S(1)} %broadcast_select_fusion.3), channel_id=1, source_target_pairs={{0,16},{1,17},{2,18},{3,19},{4,20},{5,21},{6,22},{7,23},{8,24},{9,... | collective-permute-start | bytes 983048 | tf_op jit(solution)/shard_map/while/body/eval_jaxpr/ppermute | solution.py:28
  12.8 6.8 %collective-permute-done = bf16[32,5120]{1,0:T(8,128)(2,1)S(1)} collective-permute-done((bf16[32,5120]{1,0:T(8,128)(2,1)S(1)}, bf16[32,5120]{1,0:T(8,128)(2,1)S(1)}, u32[]{:S(2)}, u32[]{:S(2)}) %collective-permute-start) | collective-permute-done | bytes 327712 | tf_op jit(solution)/shard_map/while/body/eval_jaxpr/ppermute | solution.py:28
  19.7 1.2 fusion.59
  21.2 0.4 constant_dynamic-slice_fusion.19
  21.6 1.6 collective-permute-start.2
  23.5 1.6 collective-permute-start.4
  25.2 2.5 %collective-permute-start.6 = (bf16[1,1,5120]{2,0,1:T(2,128)(2,1)S(1)}, bf16[1,1,5120]{2,0,1:T(2,128)(2,1)S(1)}, u32[]{:S(2)}, u32[]{:S(2)}) collective-permute-start(bf16[1,1,5120]{2,0,1:T(2,128)(2,1)S(1)} %get-tuple-element.585), channel_id=1, source_target_pairs={{0,6},{1,7},{2,4},{3,5},{4,2},{5,3},{6,0},{7,1},{8,14},{9,15},{10,... | collective-permute-start | bytes 30728 | tf_op jit(solution)/shard_map/while/body/eval_jaxpr/ppermute | solution.py:20
  27.9 2.6 %collective-permute-start.8 = (bf16[1,1,5120]{2,0,1:T(2,128)(2,1)S(1)}, bf16[1,1,5120]{2,0,1:T(2,128)(2,1)S(1)}, u32[]{:S(2)}, u32[]{:S(2)}) collective-permute-start(bf16[1,1,5120]{2,0,1:T(2,128)(2,1)S(1)} %get-tuple-element.587), channel_id=1, source_target_pairs={{0,8},{1,9},{2,10},{3,11},{4,12},{5,13},{6,14},{7,15},{8,0},{9,1},... | collective-permute-start | bytes 30728 | tf_op jit(solution)/shard_map/while/body/eval_jaxpr/ppermute | solution.py:20
  30.6 3.5 %collective-permute-start.10 = (bf16[1,1,5120]{2,0,1:T(2,128)(2,1)S(1)}, bf16[1,1,5120]{2,0,1:T(2,128)(2,1)S(1)}, u32[]{:S(2)}, u32[]{:S(2)}) collective-permute-start(bf16[1,1,5120]{2,0,1:T(2,128)(2,1)S(1)} %get-tuple-element.589), channel_id=1, source_target_pairs={{0,10},{1,11},{2,8},{3,9},{4,14},{5,15},{6,12},{7,13},{8,2},{9,3},... | collective-permute-start | bytes 30728 | tf_op jit(solution)/shard_map/while/body/eval_jaxpr/ppermute | solution.py:20
  34.2 3.5 %collective-permute-start.12 = (bf16[1,1,5120]{2,0,1:T(2,128)(2,1)S(1)}, bf16[1,1,5120]{2,0,1:T(2,128)(2,1)S(1)}, u32[]{:S(2)}, u32[]{:S(2)}) collective-permute-start(bf16[1,1,5120]{2,0,1:T(2,128)(2,1)S(1)} %get-tuple-element.591), channel_id=1, source_target_pairs={{0,12},{1,13},{2,14},{3,15},{4,8},{5,9},{6,10},{7,11},{8,4},{9,5},... | collective-permute-start | bytes 30728 | tf_op jit(solution)/shard_map/while/body/eval_jaxpr/ppermute | solution.py:20
  37.7 4.4 %collective-permute-start.14 = (bf16[1,1,5120]{2,0,1:T(2,128)(2,1)S(1)}, bf16[1,1,5120]{2,0,1:T(2,128)(2,1)S(1)}, u32[]{:S(2)}, u32[]{:S(2)}) collective-permute-start(bf16[1,1,5120]{2,0,1:T(2,128)(2,1)S(1)} %get-tuple-element.593), channel_id=1, source_target_pairs={{0,14},{1,15},{2,12},{3,13},{4,10},{5,11},{6,8},{7,9},{8,6},{9,7},... | collective-permute-start | bytes 30728 | tf_op jit(solution)/shard_map/while/body/eval_jaxpr/ppermute | solution.py:20
  42.3 0.3 dynamic_update_slice.244
  42.6 0.3 dynamic_update_slice.245
  42.9 0.3 dynamic_update_slice.246
  43.8 0.3 dynamic_update_slice.249
  44.1 0.3 dynamic_update_slice.250
  45.3 0.3 dynamic_update_slice.254
  45.9 0.3 dynamic_update_slice.256
  46.5 0.3 dynamic_update_slice.258
  46.8 1.3 collective-permute-done.15
  48.4 3.0 %fusion.61 = bf16[16,1,5120]{2,0,1:T(8,128)(2,1)S(1)} fusion(bf16[1,192,5120]{2,1,0:T(8,128)(2,1)} %get-tuple-element.670, bf16[16,5120]{1,0:T(8,128)(2,1)S(1)} %dynamic_update_slice.259, bf16[1,192,5120]{2,1,0:T(8,128)(2,1)S(1)} %copy-done.1), kind=kOutput, calls=%fused_computation.3.clone.1 | convolution fusion | flops 63011840 | bytes 4259840 | tf_op jit(solution)/shard_map/while/body/eval_jaxpr/dot_general | solution.py:61
  51.4 0.5 broadcast.209
  51.9 0.6 reduce.11
  52.5 0.8 reshape.326
  53.3 4.5 %all-to-all-start = ((bf16[16,2,2560]{2,1,0:T(2,128)(2,1)}), bf16[16,2,2560]{2,1,0:T(2,128)(2,1)S(1)}, u32[]{:S(2)}, u32[]{:S(2)}) async-start(bf16[16,2,2560]{2,1,0:T(2,128)(2,1)} %reshape.326), calls=%async_computation | async-start | bytes 327680 | tf_op jit(solution)/shard_map/while/body/eval_jaxpr/all_to_all | solution.py:82
  58.1 8.1 %all-to-all-done = bf16[16,2,2560]{2,1,0:T(2,128)(2,1)S(1)} async-done(((bf16[16,2,2560]{2,1,0:T(2,128)(2,1)}), bf16[16,2,2560]{2,1,0:T(2,128)(2,1)S(1)}, u32[]{:S(2)}, u32[]{:S(2)}) %all-to-all-start) | async-done | bytes 163872 | tf_op jit(solution)/shard_map/while/body/eval_jaxpr/all_to_all | solution.py:82
  66.3 0.3 reshape.328
  66.8 0.9 bitcast_select_fusion.4
  67.7 0.7 copy-done.3
  68.5 4.5 %collective-permute-start = (bf16[32,5120]{1,0:T(8,128)(2,1)S(1)}, bf16[32,5120]{1,0:T(8,128)(2,1)S(1)}, u32[]{:S(2)}, u32[]{:S(2)}) collective-permute-start(bf16[32,5120]{1,0:T(8,128)(2,1)S(1)} %broadcast_select_fusion.3), channel_id=1, source_target_pairs={{0,16},{1,17},{2,18},{3,19},{4,20},{5,21},{6,22},{7,23},{8,24},{9,... | collective-permute-start | bytes 983048 | tf_op jit(solution)/shard_map/while/body/eval_jaxpr/ppermute | solution.py:28
  73.1 6.3 %collective-permute-done = bf16[32,5120]{1,0:T(8,128)(2,1)S(1)} collective-permute-done((bf16[32,5120]{1,0:T(8,128)(2,1)S(1)}, bf16[32,5120]{1,0:T(8,128)(2,1)S(1)}, u32[]{:S(2)}, u32[]{:S(2)}) %collective-permute-start) | collective-permute-done | bytes 327712 | tf_op jit(solution)/shard_map/while/body/eval_jaxpr/ppermute | solution.py:28
  79.4 1.2 fusion.59
  80.9 0.4 constant_dynamic-slice_fusion.19
  81.3 0.8 collective-permute-start.2
  82.1 1.1 collective-permute-start.3
  83.2 0.9 collective-permute-start.4
  84.1 0.8 collective-permute-start.5
  84.9 1.1 collective-permute-start.6
  86.0 1.6 collective-permute-start.7
  87.6 1.0 collective-permute-start.8
  88.5 1.6 %collective-permute-start.9 = (bf16[1,1,5120]{2,0,1:T(2,128)(2,1)S(1)}, bf16[1,1,5120]{2,0,1:T(2,128)(2,1)S(1)}, u32[]{:S(2)}, u32[]{:S(2)}) collective-permute-start(bf16[1,1,5120]{2,0,1:T(2,128)(2,1)S(1)} %get-tuple-element.588), channel_id=1, source_target_pairs={{0,9},{1,8},{2,11},{3,10},{4,13},{5,12},{6,15},{7,14},{8,1},{9,0},... | collective-permute-start | bytes 30728 | tf_op jit(solution)/shard_map/while/body/eval_jaxpr/ppermute | solution.py:20
  90.2 1.1 collective-permute-start.10
  91.3 2.4 %collective-permute-start.11 = (bf16[1,1,5120]{2,0,1:T(2,128)(2,1)S(1)}, bf16[1,1,5120]{2,0,1:T(2,128)(2,1)S(1)}, u32[]{:S(2)}, u32[]{:S(2)}) collective-permute-start(bf16[1,1,5120]{2,0,1:T(2,128)(2,1)S(1)} %get-tuple-element.590), channel_id=1, source_target_pairs={{0,11},{1,10},{2,9},{3,8},{4,15},{5,14},{6,13},{7,12},{8,3},{9,2},... | collective-permute-start | bytes 30728 | tf_op jit(solution)/shard_map/while/body/eval_jaxpr/ppermute | solution.py:20
  93.8 1.8 %collective-permute-start.12 = (bf16[1,1,5120]{2,0,1:T(2,128)(2,1)S(1)}, bf16[1,1,5120]{2,0,1:T(2,128)(2,1)S(1)}, u32[]{:S(2)}, u32[]{:S(2)}) collective-permute-start(bf16[1,1,5120]{2,0,1:T(2,128)(2,1)S(1)} %get-tuple-element.591), channel_id=1, source_target_pairs={{0,12},{1,13},{2,14},{3,15},{4,8},{5,9},{6,10},{7,11},{8,4},{9,5},... | collective-permute-start | bytes 30728 | tf_op jit(solution)/shard_map/while/body/eval_jaxpr/ppermute | solution.py:20
  95.6 1.7 %collective-permute-start.13 = (bf16[1,1,5120]{2,0,1:T(2,128)(2,1)S(1)}, bf16[1,1,5120]{2,0,1:T(2,128)(2,1)S(1)}, u32[]{:S(2)}, u32[]{:S(2)}) collective-permute-start(bf16[1,1,5120]{2,0,1:T(2,128)(2,1)S(1)} %get-tuple-element.592), channel_id=1, source_target_pairs={{0,13},{1,12},{2,15},{3,14},{4,9},{5,8},{6,11},{7,10},{8,5},{9,4},... | collective-permute-start | bytes 30728 | tf_op jit(solution)/shard_map/while/body/eval_jaxpr/ppermute | solution.py:20
  97.3 2.0 %collective-permute-start.14 = (bf16[1,1,5120]{2,0,1:T(2,128)(2,1)S(1)}, bf16[1,1,5120]{2,0,1:T(2,128)(2,1)S(1)}, u32[]{:S(2)}, u32[]{:S(2)}) collective-permute-start(bf16[1,1,5120]{2,0,1:T(2,128)(2,1)S(1)} %get-tuple-element.593), channel_id=1, source_target_pairs={{0,14},{1,15},{2,12},{3,13},{4,10},{5,11},{6,8},{7,9},{8,6},{9,7},... | collective-permute-start | bytes 30728 | tf_op jit(solution)/shard_map/while/body/eval_jaxpr/ppermute | solution.py:20
  99.3 2.5 %collective-permute-start.15 = (bf16[1,1,5120]{2,0,1:T(2,128)(2,1)S(1)}, bf16[1,1,5120]{2,0,1:T(2,128)(2,1)S(1)}, u32[]{:S(2)}, u32[]{:S(2)}) collective-permute-start(bf16[1,1,5120]{2,0,1:T(2,128)(2,1)S(1)} %get-tuple-element.594), channel_id=1, source_target_pairs={{0,15},{1,14},{2,13},{3,12},{4,11},{5,10},{6,9},{7,8},{8,7},{9,6},... | collective-permute-start | bytes 30728 | tf_op jit(solution)/shard_map/while/body/eval_jaxpr/ppermute | solution.py:20
  101.8 0.3 dynamic_update_slice.244
  103.0 0.3 dynamic_update_slice.248
  106.6 3.0 %fusion.61 = bf16[16,1,5120]{2,0,1:T(8,128)(2,1)S(1)} fusion(bf16[1,192,5120]{2,1,0:T(8,128)(2,1)} %get-tuple-element.670, bf16[16,5120]{1,0:T(8,128)(2,1)S(1)} %dynamic_update_slice.259, bf16[1,192,5120]{2,1,0:T(8,128)(2,1)S(1)} %copy-done.1), kind=kOutput, calls=%fused_computation.3.clone.1 | convolution fusion | flops 63011840 | bytes 4259840 | tf_op jit(solution)/shard_map/while/body/eval_jaxpr/dot_general | solution.py:61
  109.6 0.5 broadcast.209
  110.1 0.6 reduce.11
  110.8 0.8 reshape.326
  111.5 3.5 %all-to-all-start = ((bf16[16,2,2560]{2,1,0:T(2,128)(2,1)}), bf16[16,2,2560]{2,1,0:T(2,128)(2,1)S(1)}, u32[]{:S(2)}, u32[]{:S(2)}) async-start(bf16[16,2,2560]{2,1,0:T(2,128)(2,1)} %reshape.326), calls=%async_computation | async-start | bytes 327680 | tf_op jit(solution)/shard_map/while/body/eval_jaxpr/all_to_all | solution.py:82
  115.3 8.1 %all-to-all-done = bf16[16,2,2560]{2,1,0:T(2,128)(2,1)S(1)} async-done(((bf16[16,2,2560]{2,1,0:T(2,128)(2,1)}), bf16[16,2,2560]{2,1,0:T(2,128)(2,1)S(1)}, u32[]{:S(2)}, u32[]{:S(2)}) %all-to-all-start) | async-done | bytes 163872 | tf_op jit(solution)/shard_map/while/body/eval_jaxpr/all_to_all | solution.py:82
  123.6 0.3 reshape.328
  124.1 0.9 bitcast_select_fusion.4
  125.0 0.7 copy-done.3
  125.7 0.8 broadcast_select_fusion.1
  126.5 24.3 %all-reduce.2.cloned.1.call-done = bf16[1,32,5120]{2,1,0:T(8,128)(2,1)} async-done(((bf16[1,32,5120]{2,1,0:T(8,128)(2,1)}), bf16[1,32,5120]{2,1,0:T(8,128)(2,1)}) %all-reduce.2.cloned.1.call-update) | async-done | bytes 327696 | tf_op jit(solution)/shard_map/psum | solution.py:33
  150.7 1.1 fusion.23
  151.9 1.9 %fusion.22 = bf16[1,1,32,64]{3,2,1,0:T(8,128)(2,1)} fusion(bf16[1,64,5120]{2,1,0:T(8,128)(2,1)S(1)} %copy-done, bf16[1,32,5120]{2,1,0:T(8,128)(2,1)} %all-reduce.2.cloned.1.call-done, f32[32]{0:T(128)S(1)} %add_rsqrt_fusion.1), kind=kOutput, calls=%fused_computation.47 | convolution fusion | flops 21465088 | bytes 987264 | tf_op jit(solution)/shard_map/mtd,jd->mtj/dot_general | solution.py:113
  (103 shorter events, 9.6 us)
Async XLA Ops:
  6.5 145.4 %copy-start = (bf16[1,64,5120]{2,1,0:T(8,128)(2,1)S(1)}, bf16[1,64,5120]{2,1,0:T(8,128)(2,1)}, u32[]{:S(2)}) copy-start(bf16[1,64,5120]{2,1,0:T(8,128)(2,1)} %param.13) | copy-start | bytes 1966084
  6.5 144.2 %all-reduce.2.cloned.1.call-start = ((), (), s32[]{:S(2)}) async-start(), calls=%async_computation.1 | async-start | bytes 655360 | tf_op jit(solution)/shard_map/psum | solution.py:33
  7.7 40.7 %copy-start.1 = (bf16[1,192,5120]{2,1,0:T(8,128)(2,1)S(1)}, bf16[1,192,5120]{2,1,0:T(8,128)(2,1)}, u32[]{:S(2)}) copy-start(bf16[1,192,5120]{2,1,0:T(8,128)(2,1)} %get-tuple-element.669) | copy-start | bytes 5898244 | tf_op jit(solution)/shard_map/while
  7.7 12.0 %collective-permute-start = (bf16[32,5120]{1,0:T(8,128)(2,1)S(1)}, bf16[32,5120]{1,0:T(8,128)(2,1)S(1)}, u32[]{:S(2)}, u32[]{:S(2)}) collective-permute-start(bf16[32,5120]{1,0:T(8,128)(2,1)S(1)} %broadcast_select_fusion.3), channel_id=1, source_target_pairs={{0,16},{1,17},{2,18},{3,19},{4,20},{5,21},{6,22},{7,23},{8,24},{9,... | collective-permute-start | bytes 983048 | tf_op jit(solution)/shard_map/while/body/eval_jaxpr/ppermute | solution.py:28
  21.6 3.6 %collective-permute-start.1 = (bf16[1,1,5120]{2,0,1:T(2,128)(2,1)S(1)}, bf16[1,1,5120]{2,0,1:T(2,128)(2,1)S(1)}, u32[]{:S(2)}, u32[]{:S(2)}) collective-permute-start(bf16[1,1,5120]{2,0,1:T(2,128)(2,1)S(1)} %get-tuple-element.580), channel_id=1, source_target_pairs={{0,1},{1,0},{2,3},{3,2},{4,5},{5,4},{6,7},{7,6},{8,9},{9,8},{10,11... | collective-permute-start | bytes 30728 | tf_op jit(solution)/shard_map/while/body/eval_jaxpr/ppermute | solution.py:20
  21.6 6.1 %collective-permute-start.2 = (bf16[1,1,5120]{2,0,1:T(2,128)(2,1)S(1)}, bf16[1,1,5120]{2,0,1:T(2,128)(2,1)S(1)}, u32[]{:S(2)}, u32[]{:S(2)}) collective-permute-start(bf16[1,1,5120]{2,0,1:T(2,128)(2,1)S(1)} %get-tuple-element.581), channel_id=1, source_target_pairs={{0,2},{1,3},{2,0},{3,1},{4,6},{5,7},{6,4},{7,5},{8,10},{9,11},{10,... | collective-permute-start | bytes 30728 | tf_op jit(solution)/shard_map/while/body/eval_jaxpr/ppermute | solution.py:20
  23.2 4.7 %collective-permute-start.3 = (bf16[1,1,5120]{2,0,1:T(2,128)(2,1)S(1)}, bf16[1,1,5120]{2,0,1:T(2,128)(2,1)S(1)}, u32[]{:S(2)}, u32[]{:S(2)}) collective-permute-start(bf16[1,1,5120]{2,0,1:T(2,128)(2,1)S(1)} %get-tuple-element.582), channel_id=1, source_target_pairs={{0,3},{1,2},{2,1},{3,0},{4,7},{5,6},{6,5},{7,4},{8,11},{9,10},{10,... | collective-permute-start | bytes 30728 | tf_op jit(solution)/shard_map/while/body/eval_jaxpr/ppermute | solution.py:20
  23.5 7.0 %collective-permute-start.4 = (bf16[1,1,5120]{2,0,1:T(2,128)(2,1)S(1)}, bf16[1,1,5120]{2,0,1:T(2,128)(2,1)S(1)}, u32[]{:S(2)}, u32[]{:S(2)}) collective-permute-start(bf16[1,1,5120]{2,0,1:T(2,128)(2,1)S(1)} %get-tuple-element.583), channel_id=1, source_target_pairs={{0,4},{1,5},{2,6},{3,7},{4,0},{5,1},{6,2},{7,3},{8,12},{9,13},{10,... | collective-permute-start | bytes 30728 | tf_op jit(solution)/shard_map/while/body/eval_jaxpr/ppermute | solution.py:20
  25.1 5.5 %collective-permute-start.5 = (bf16[1,1,5120]{2,0,1:T(2,128)(2,1)S(1)}, bf16[1,1,5120]{2,0,1:T(2,128)(2,1)S(1)}, u32[]{:S(2)}, u32[]{:S(2)}) collective-permute-start(bf16[1,1,5120]{2,0,1:T(2,128)(2,1)S(1)} %get-tuple-element.584), channel_id=1, source_target_pairs={{0,5},{1,4},{2,7},{3,6},{4,1},{5,0},{6,3},{7,2},{8,13},{9,12},{10,... | collective-permute-start | bytes 30728 | tf_op jit(solution)/shard_map/while/body/eval_jaxpr/ppermute | solution.py:20
  25.2 8.9 %collective-permute-start.6 = (bf16[1,1,5120]{2,0,1:T(2,128)(2,1)S(1)}, bf16[1,1,5120]{2,0,1:T(2,128)(2,1)S(1)}, u32[]{:S(2)}, u32[]{:S(2)}) collective-permute-start(bf16[1,1,5120]{2,0,1:T(2,128)(2,1)S(1)} %get-tuple-element.585), channel_id=1, source_target_pairs={{0,6},{1,7},{2,4},{3,5},{4,2},{5,3},{6,0},{7,1},{8,14},{9,15},{10,... | collective-permute-start | bytes 30728 | tf_op jit(solution)/shard_map/while/body/eval_jaxpr/ppermute | solution.py:20
  27.7 6.4 %collective-permute-start.7 = (bf16[1,1,5120]{2,0,1:T(2,128)(2,1)S(1)}, bf16[1,1,5120]{2,0,1:T(2,128)(2,1)S(1)}, u32[]{:S(2)}, u32[]{:S(2)}) collective-permute-start(bf16[1,1,5120]{2,0,1:T(2,128)(2,1)S(1)} %get-tuple-element.586), channel_id=1, source_target_pairs={{0,7},{1,6},{2,5},{3,4},{4,3},{5,2},{6,1},{7,0},{8,15},{9,14},{10,... | collective-permute-start | bytes 30728 | tf_op jit(solution)/shard_map/while/body/eval_jaxpr/ppermute | solution.py:20
  27.9 9.8 %collective-permute-start.8 = (bf16[1,1,5120]{2,0,1:T(2,128)(2,1)S(1)}, bf16[1,1,5120]{2,0,1:T(2,128)(2,1)S(1)}, u32[]{:S(2)}, u32[]{:S(2)}) collective-permute-start(bf16[1,1,5120]{2,0,1:T(2,128)(2,1)S(1)} %get-tuple-element.587), channel_id=1, source_target_pairs={{0,8},{1,9},{2,10},{3,11},{4,12},{5,13},{6,14},{7,15},{8,0},{9,1},... | collective-permute-start | bytes 30728 | tf_op jit(solution)/shard_map/while/body/eval_jaxpr/ppermute | solution.py:20
  30.5 7.3 %collective-permute-start.9 = (bf16[1,1,5120]{2,0,1:T(2,128)(2,1)S(1)}, bf16[1,1,5120]{2,0,1:T(2,128)(2,1)S(1)}, u32[]{:S(2)}, u32[]{:S(2)}) collective-permute-start(bf16[1,1,5120]{2,0,1:T(2,128)(2,1)S(1)} %get-tuple-element.588), channel_id=1, source_target_pairs={{0,9},{1,8},{2,11},{3,10},{4,13},{5,12},{6,15},{7,14},{8,1},{9,0},... | collective-permute-start | bytes 30728 | tf_op jit(solution)/shard_map/while/body/eval_jaxpr/ppermute | solution.py:20
  30.6 11.6 %collective-permute-start.10 = (bf16[1,1,5120]{2,0,1:T(2,128)(2,1)S(1)}, bf16[1,1,5120]{2,0,1:T(2,128)(2,1)S(1)}, u32[]{:S(2)}, u32[]{:S(2)}) collective-permute-start(bf16[1,1,5120]{2,0,1:T(2,128)(2,1)S(1)} %get-tuple-element.589), channel_id=1, source_target_pairs={{0,10},{1,11},{2,8},{3,9},{4,14},{5,15},{6,12},{7,13},{8,2},{9,3},... | collective-permute-start | bytes 30728 | tf_op jit(solution)/shard_map/while/body/eval_jaxpr/ppermute | solution.py:20
  34.1 11.5 %collective-permute-start.11 = (bf16[1,1,5120]{2,0,1:T(2,128)(2,1)S(1)}, bf16[1,1,5120]{2,0,1:T(2,128)(2,1)S(1)}, u32[]{:S(2)}, u32[]{:S(2)}) collective-permute-start(bf16[1,1,5120]{2,0,1:T(2,128)(2,1)S(1)} %get-tuple-element.590), channel_id=1, source_target_pairs={{0,11},{1,10},{2,9},{3,8},{4,15},{5,14},{6,13},{7,12},{8,3},{9,2},... | collective-permute-start | bytes 30728 | tf_op jit(solution)/shard_map/while/body/eval_jaxpr/ppermute | solution.py:20
  34.2 11.7 %collective-permute-start.12 = (bf16[1,1,5120]{2,0,1:T(2,128)(2,1)S(1)}, bf16[1,1,5120]{2,0,1:T(2,128)(2,1)S(1)}, u32[]{:S(2)}, u32[]{:S(2)}) collective-permute-start(bf16[1,1,5120]{2,0,1:T(2,128)(2,1)S(1)} %get-tuple-element.591), channel_id=1, source_target_pairs={{0,12},{1,13},{2,14},{3,15},{4,8},{5,9},{6,10},{7,11},{8,4},{9,5},... | collective-permute-start | bytes 30728 | tf_op jit(solution)/shard_map/while/body/eval_jaxpr/ppermute | solution.py:20
  37.7 8.5 %collective-permute-start.13 = (bf16[1,1,5120]{2,0,1:T(2,128)(2,1)S(1)}, bf16[1,1,5120]{2,0,1:T(2,128)(2,1)S(1)}, u32[]{:S(2)}, u32[]{:S(2)}) collective-permute-start(bf16[1,1,5120]{2,0,1:T(2,128)(2,1)S(1)} %get-tuple-element.592), channel_id=1, source_target_pairs={{0,13},{1,12},{2,15},{3,14},{4,9},{5,8},{6,11},{7,10},{8,5},{9,4},... | collective-permute-start | bytes 30728 | tf_op jit(solution)/shard_map/while/body/eval_jaxpr/ppermute | solution.py:20
  37.7 8.7 %collective-permute-start.14 = (bf16[1,1,5120]{2,0,1:T(2,128)(2,1)S(1)}, bf16[1,1,5120]{2,0,1:T(2,128)(2,1)S(1)}, u32[]{:S(2)}, u32[]{:S(2)}) collective-permute-start(bf16[1,1,5120]{2,0,1:T(2,128)(2,1)S(1)} %get-tuple-element.593), channel_id=1, source_target_pairs={{0,14},{1,15},{2,12},{3,13},{4,10},{5,11},{6,8},{7,9},{8,6},{9,7},... | collective-permute-start | bytes 30728 | tf_op jit(solution)/shard_map/while/body/eval_jaxpr/ppermute | solution.py:20
  42.2 5.9 %collective-permute-start.15 = (bf16[1,1,5120]{2,0,1:T(2,128)(2,1)S(1)}, bf16[1,1,5120]{2,0,1:T(2,128)(2,1)S(1)}, u32[]{:S(2)}, u32[]{:S(2)}) collective-permute-start(bf16[1,1,5120]{2,0,1:T(2,128)(2,1)S(1)} %get-tuple-element.594), channel_id=1, source_target_pairs={{0,15},{1,14},{2,13},{3,12},{4,11},{5,10},{6,9},{7,8},{8,7},{9,6},... | collective-permute-start | bytes 30728 | tf_op jit(solution)/shard_map/while/body/eval_jaxpr/ppermute | solution.py:20
  48.3 9.5 %copy-start.4 = (bf16[1,5120,2]{1,2,0:T(2,128)(2,1)S(1)}, bf16[1,5120,2]{1,2,0:T(2,128)(2,1)}, u32[]{:S(2)}) copy-start(bf16[1,5120,2]{1,2,0:T(2,128)(2,1)} %get-tuple-element.666) | copy-start | bytes 61444 | tf_op jit(solution)/shard_map/while
  51.4 15.4 %copy-start.2 = (bf16[1,32,5120]{2,1,0:T(8,128)(2,1)S(1)}, bf16[1,32,5120]{2,1,0:T(8,128)(2,1)}, u32[]{:S(2)}) copy-start(bf16[1,32,5120]{2,1,0:T(8,128)(2,1)} %get-tuple-element.631) | copy-start | bytes 983044 | tf_op jit(solution)/shard_map/while
  53.3 12.9 %all-to-all-start = ((bf16[16,2,2560]{2,1,0:T(2,128)(2,1)}), bf16[16,2,2560]{2,1,0:T(2,128)(2,1)S(1)}, u32[]{:S(2)}, u32[]{:S(2)}) async-start(bf16[16,2,2560]{2,1,0:T(2,128)(2,1)} %reshape.326), calls=%async_computation | async-start | bytes 327680 | tf_op jit(solution)/shard_map/while/body/eval_jaxpr/all_to_all | solution.py:82
  67.7 0.7 copy-start.3
  68.4 38.1 %copy-start.1 = (bf16[1,192,5120]{2,1,0:T(8,128)(2,1)S(1)}, bf16[1,192,5120]{2,1,0:T(8,128)(2,1)}, u32[]{:S(2)}) copy-start(bf16[1,192,5120]{2,1,0:T(8,128)(2,1)} %get-tuple-element.669) | copy-start | bytes 5898244 | tf_op jit(solution)/shard_map/while
  68.5 10.9 %collective-permute-start = (bf16[32,5120]{1,0:T(8,128)(2,1)S(1)}, bf16[32,5120]{1,0:T(8,128)(2,1)S(1)}, u32[]{:S(2)}, u32[]{:S(2)}) collective-permute-start(bf16[32,5120]{1,0:T(8,128)(2,1)S(1)} %broadcast_select_fusion.3), channel_id=1, source_target_pairs={{0,16},{1,17},{2,18},{3,19},{4,20},{5,21},{6,22},{7,23},{8,24},{9,... | collective-permute-start | bytes 983048 | tf_op jit(solution)/shard_map/while/body/eval_jaxpr/ppermute | solution.py:28
  81.2 3.6 %collective-permute-start.1 = (bf16[1,1,5120]{2,0,1:T(2,128)(2,1)S(1)}, bf16[1,1,5120]{2,0,1:T(2,128)(2,1)S(1)}, u32[]{:S(2)}, u32[]{:S(2)}) collective-permute-start(bf16[1,1,5120]{2,0,1:T(2,128)(2,1)S(1)} %get-tuple-element.580), channel_id=1, source_target_pairs={{0,1},{1,0},{2,3},{3,2},{4,5},{5,4},{6,7},{7,6},{8,9},{9,8},{10,11... | collective-permute-start | bytes 30728 | tf_op jit(solution)/shard_map/while/body/eval_jaxpr/ppermute | solution.py:20
  81.3 4.7 %collective-permute-start.2 = (bf16[1,1,5120]{2,0,1:T(2,128)(2,1)S(1)}, bf16[1,1,5120]{2,0,1:T(2,128)(2,1)S(1)}, u32[]{:S(2)}, u32[]{:S(2)}) collective-permute-start(bf16[1,1,5120]{2,0,1:T(2,128)(2,1)S(1)} %get-tuple-element.581), channel_id=1, source_target_pairs={{0,2},{1,3},{2,0},{3,1},{4,6},{5,7},{6,4},{7,5},{8,10},{9,11},{10,... | collective-permute-start | bytes 30728 | tf_op jit(solution)/shard_map/while/body/eval_jaxpr/ppermute | solution.py:20
  82.1 5.5 %collective-permute-start.3 = (bf16[1,1,5120]{2,0,1:T(2,128)(2,1)S(1)}, bf16[1,1,5120]{2,0,1:T(2,128)(2,1)S(1)}, u32[]{:S(2)}, u32[]{:S(2)}) collective-permute-start(bf16[1,1,5120]{2,0,1:T(2,128)(2,1)S(1)} %get-tuple-element.582), channel_id=1, source_target_pairs={{0,3},{1,2},{2,1},{3,0},{4,7},{5,6},{6,5},{7,4},{8,11},{9,10},{10,... | collective-permute-start | bytes 30728 | tf_op jit(solution)/shard_map/while/body/eval_jaxpr/ppermute | solution.py:20
  83.2 5.4 %collective-permute-start.4 = (bf16[1,1,5120]{2,0,1:T(2,128)(2,1)S(1)}, bf16[1,1,5120]{2,0,1:T(2,128)(2,1)S(1)}, u32[]{:S(2)}, u32[]{:S(2)}) collective-permute-start(bf16[1,1,5120]{2,0,1:T(2,128)(2,1)S(1)} %get-tuple-element.583), channel_id=1, source_target_pairs={{0,4},{1,5},{2,6},{3,7},{4,0},{5,1},{6,2},{7,3},{8,12},{9,13},{10,... | collective-permute-start | bytes 30728 | tf_op jit(solution)/shard_map/while/body/eval_jaxpr/ppermute | solution.py:20
  84.1 6.1 %collective-permute-start.5 = (bf16[1,1,5120]{2,0,1:T(2,128)(2,1)S(1)}, bf16[1,1,5120]{2,0,1:T(2,128)(2,1)S(1)}, u32[]{:S(2)}, u32[]{:S(2)}) collective-permute-start(bf16[1,1,5120]{2,0,1:T(2,128)(2,1)S(1)} %get-tuple-element.584), channel_id=1, source_target_pairs={{0,5},{1,4},{2,7},{3,6},{4,1},{5,0},{6,3},{7,2},{8,13},{9,12},{10,... | collective-permute-start | bytes 30728 | tf_op jit(solution)/shard_map/while/body/eval_jaxpr/ppermute | solution.py:20
  84.9 6.4 %collective-permute-start.6 = (bf16[1,1,5120]{2,0,1:T(2,128)(2,1)S(1)}, bf16[1,1,5120]{2,0,1:T(2,128)(2,1)S(1)}, u32[]{:S(2)}, u32[]{:S(2)}) collective-permute-start(bf16[1,1,5120]{2,0,1:T(2,128)(2,1)S(1)} %get-tuple-element.585), channel_id=1, source_target_pairs={{0,6},{1,7},{2,4},{3,5},{4,2},{5,3},{6,0},{7,1},{8,14},{9,15},{10,... | collective-permute-start | bytes 30728 | tf_op jit(solution)/shard_map/while/body/eval_jaxpr/ppermute | solution.py:20
  86.0 7.8 %collective-permute-start.7 = (bf16[1,1,5120]{2,0,1:T(2,128)(2,1)S(1)}, bf16[1,1,5120]{2,0,1:T(2,128)(2,1)S(1)}, u32[]{:S(2)}, u32[]{:S(2)}) collective-permute-start(bf16[1,1,5120]{2,0,1:T(2,128)(2,1)S(1)} %get-tuple-element.586), channel_id=1, source_target_pairs={{0,7},{1,6},{2,5},{3,4},{4,3},{5,2},{6,1},{7,0},{8,15},{9,14},{10,... | collective-permute-start | bytes 30728 | tf_op jit(solution)/shard_map/while/body/eval_jaxpr/ppermute | solution.py:20
  87.6 8.0 %collective-permute-start.8 = (bf16[1,1,5120]{2,0,1:T(2,128)(2,1)S(1)}, bf16[1,1,5120]{2,0,1:T(2,128)(2,1)S(1)}, u32[]{:S(2)}, u32[]{:S(2)}) collective-permute-start(bf16[1,1,5120]{2,0,1:T(2,128)(2,1)S(1)} %get-tuple-element.587), channel_id=1, source_target_pairs={{0,8},{1,9},{2,10},{3,11},{4,12},{5,13},{6,14},{7,15},{8,0},{9,1},... | collective-permute-start | bytes 30728 | tf_op jit(solution)/shard_map/while/body/eval_jaxpr/ppermute | solution.py:20
  88.5 8.8 %collective-permute-start.9 = (bf16[1,1,5120]{2,0,1:T(2,128)(2,1)S(1)}, bf16[1,1,5120]{2,0,1:T(2,128)(2,1)S(1)}, u32[]{:S(2)}, u32[]{:S(2)}) collective-permute-start(bf16[1,1,5120]{2,0,1:T(2,128)(2,1)S(1)} %get-tuple-element.588), channel_id=1, source_target_pairs={{0,9},{1,8},{2,11},{3,10},{4,13},{5,12},{6,15},{7,14},{8,1},{9,0},... | collective-permute-start | bytes 30728 | tf_op jit(solution)/shard_map/while/body/eval_jaxpr/ppermute | solution.py:20
  90.2 9.1 %collective-permute-start.10 = (bf16[1,1,5120]{2,0,1:T(2,128)(2,1)S(1)}, bf16[1,1,5120]{2,0,1:T(2,128)(2,1)S(1)}, u32[]{:S(2)}, u32[]{:S(2)}) collective-permute-start(bf16[1,1,5120]{2,0,1:T(2,128)(2,1)S(1)} %get-tuple-element.589), channel_id=1, source_target_pairs={{0,10},{1,11},{2,8},{3,9},{4,14},{5,15},{6,12},{7,13},{8,2},{9,3},... | collective-permute-start | bytes 30728 | tf_op jit(solution)/shard_map/while/body/eval_jaxpr/ppermute | solution.py:20
  91.3 13.7 %collective-permute-start.11 = (bf16[1,1,5120]{2,0,1:T(2,128)(2,1)S(1)}, bf16[1,1,5120]{2,0,1:T(2,128)(2,1)S(1)}, u32[]{:S(2)}, u32[]{:S(2)}) collective-permute-start(bf16[1,1,5120]{2,0,1:T(2,128)(2,1)S(1)} %get-tuple-element.590), channel_id=1, source_target_pairs={{0,11},{1,10},{2,9},{3,8},{4,15},{5,14},{6,13},{7,12},{8,3},{9,2},... | collective-permute-start | bytes 30728 | tf_op jit(solution)/shard_map/while/body/eval_jaxpr/ppermute | solution.py:20
  93.8 11.6 %collective-permute-start.12 = (bf16[1,1,5120]{2,0,1:T(2,128)(2,1)S(1)}, bf16[1,1,5120]{2,0,1:T(2,128)(2,1)S(1)}, u32[]{:S(2)}, u32[]{:S(2)}) collective-permute-start(bf16[1,1,5120]{2,0,1:T(2,128)(2,1)S(1)} %get-tuple-element.591), channel_id=1, source_target_pairs={{0,12},{1,13},{2,14},{3,15},{4,8},{5,9},{6,10},{7,11},{8,4},{9,5},... | collective-permute-start | bytes 30728 | tf_op jit(solution)/shard_map/while/body/eval_jaxpr/ppermute | solution.py:20
  95.6 10.1 %collective-permute-start.13 = (bf16[1,1,5120]{2,0,1:T(2,128)(2,1)S(1)}, bf16[1,1,5120]{2,0,1:T(2,128)(2,1)S(1)}, u32[]{:S(2)}, u32[]{:S(2)}) collective-permute-start(bf16[1,1,5120]{2,0,1:T(2,128)(2,1)S(1)} %get-tuple-element.592), channel_id=1, source_target_pairs={{0,13},{1,12},{2,15},{3,14},{4,9},{5,8},{6,11},{7,10},{8,5},{9,4},... | collective-permute-start | bytes 30728 | tf_op jit(solution)/shard_map/while/body/eval_jaxpr/ppermute | solution.py:20
  97.3 8.7 %collective-permute-start.14 = (bf16[1,1,5120]{2,0,1:T(2,128)(2,1)S(1)}, bf16[1,1,5120]{2,0,1:T(2,128)(2,1)S(1)}, u32[]{:S(2)}, u32[]{:S(2)}) collective-permute-start(bf16[1,1,5120]{2,0,1:T(2,128)(2,1)S(1)} %get-tuple-element.593), channel_id=1, source_target_pairs={{0,14},{1,15},{2,12},{3,13},{4,10},{5,11},{6,8},{7,9},{8,6},{9,7},... | collective-permute-start | bytes 30728 | tf_op jit(solution)/shard_map/while/body/eval_jaxpr/ppermute | solution.py:20
  99.3 7.0 %collective-permute-start.15 = (bf16[1,1,5120]{2,0,1:T(2,128)(2,1)S(1)}, bf16[1,1,5120]{2,0,1:T(2,128)(2,1)S(1)}, u32[]{:S(2)}, u32[]{:S(2)}) collective-permute-start(bf16[1,1,5120]{2,0,1:T(2,128)(2,1)S(1)} %get-tuple-element.594), channel_id=1, source_target_pairs={{0,15},{1,14},{2,13},{3,12},{4,11},{5,10},{6,9},{7,8},{8,7},{9,6},... | collective-permute-start | bytes 30728 | tf_op jit(solution)/shard_map/while/body/eval_jaxpr/ppermute | solution.py:20
  106.6 8.5 %copy-start.4 = (bf16[1,5120,2]{1,2,0:T(2,128)(2,1)S(1)}, bf16[1,5120,2]{1,2,0:T(2,128)(2,1)}, u32[]{:S(2)}) copy-start(bf16[1,5120,2]{1,2,0:T(2,128)(2,1)} %get-tuple-element.666) | copy-start | bytes 61444 | tf_op jit(solution)/shard_map/while
  109.6 14.4 %copy-start.2 = (bf16[1,32,5120]{2,1,0:T(8,128)(2,1)S(1)}, bf16[1,32,5120]{2,1,0:T(8,128)(2,1)}, u32[]{:S(2)}) copy-start(bf16[1,32,5120]{2,1,0:T(8,128)(2,1)} %get-tuple-element.631) | copy-start | bytes 983044 | tf_op jit(solution)/shard_map/while
  111.5 11.9 %all-to-all-start = ((bf16[16,2,2560]{2,1,0:T(2,128)(2,1)}), bf16[16,2,2560]{2,1,0:T(2,128)(2,1)S(1)}, u32[]{:S(2)}, u32[]{:S(2)}) async-start(bf16[16,2,2560]{2,1,0:T(2,128)(2,1)} %reshape.326), calls=%async_computation | async-start | bytes 327680 | tf_op jit(solution)/shard_map/while/body/eval_jaxpr/all_to_all | solution.py:82
  124.9 0.7 copy-start.3
Sparse Core Ops, SparseCore 0:
  126.6 24.1 all-reduce.1
